TPU v7x, 32 devices: a whole 2x2x4 slice. The times are simulated.
32 devices in a mesh: row: 8 (over z, y), col: 4 (over x, core).
Axes of the slice: x: 2, y: 2, z: 4, core: 2. Of those that a mesh axis runs over, the one named last changes fastest.
Arguments:
- state: float32 [2, 8192, 8192], P(None, 'row', 'col'), as said below
- tile_vals: float32 [64, 2, 128, 128], P(('row', 'col')), may hold values from -0.375 to 0.375
- tile_row: int32 [64], P(('row', 'col')), may hold values from 0 to 63, as said below
- tile_col: int32 [64], P(('row', 'col')), may hold values from 0 to 63, as said below
- tile_op: int32 [64], P(('row', 'col')), may hold values from 0 to 16, as said below
Outputs:
- evolved: float32 [2, 8192, 8192], P(None, 'row', 'col')
Inputs may be any that keep to these rules, and one draw needn't show every extreme that they name: Hermitian: state[0] is symmetric and state[1] antisymmetric. `tile_row`: in each aligned block of 8 entries (the tiles stored on the devices of one index of row), at most 2 lie in any one row slab, the tile rows 8 * s to 8 * s + 7 for s < 8. tile_col equals tile_row or tile_row + 1. `tile_op`: value 16 marks the effective Hamiltonian, smaller values the jump operators. Among the tiles whose rows lie in one row slab, at most 2 carry any one value.
All inputs are finite; a program needn't handle non-finite values.
Results may differ from a plain program's by a relative error of at most 0.0001.
Values sent between devices are 32-bit elements; how exact they have to be, the bound alone decides.
No kernel may reach another device: no remote copies, remote signals or barrier semaphores. Data moves between devices by JAX's collectives and lax.ppermute only.
A program may use at most 256 MiB of HBM per device.

v0:
```python
import jax
import jax.numpy as jnp
from jax import lax
from jax.sharding import PartitionSpec as P

NOPS = 16
CAP = 2
PRECISE = lax.Precision.HIGHEST
TIME_STEP = 0.25


def from_root(value, axis, source):
    kept = jnp.where(lax.axis_index(axis) == source, value, 0).astype(value.dtype)
    return lax.psum(kept, axis)


def passed_along(block, axis, distance):
    devices = range(lax.axis_size(axis))
    route = [(i - distance, i) for i in devices if i - distance in devices]
    return lax.ppermute(block, axis, route)


def complex_product(formula, left_part, right_part):
    real_prod = jnp.einsum(
        formula, left_part[0], right_part[0], precision=PRECISE, preferred_element_type=jnp.float32
    )
    imag_prod = jnp.einsum(
        formula, left_part[1], right_part[1], precision=PRECISE, preferred_element_type=jnp.float32
    )
    mixed_prod = jnp.einsum(
        formula,
        left_part[0] + left_part[1],
        right_part[0] + right_part[1],
        precision=PRECISE,
        preferred_element_type=jnp.float32,
    )
    return jnp.stack([real_prod - imag_prod, mixed_prod - real_prod - imag_prod])


def adjoint(tile_set):
    return jnp.stack([jnp.swapaxes(tile_set[0], -1, -2), -jnp.swapaxes(tile_set[1], -1, -2)])


def times_minus_i(values):
    return jnp.stack([values[1], -values[0]])


def times_i(values):
    return jnp.stack([-values[1], values[0]])


def compact(tile_set, row_ids, col_ids, op_ids, capacity, kind_count):
    slot_total = op_ids.shape[0]
    position = jnp.arange(slot_total, dtype=jnp.int32)
    earlier = (op_ids[:, None] == op_ids[None, :]) & (position[None, :] < position[:, None])
    rank_ids = jnp.sum(earlier.astype(jnp.int32), axis=1, dtype=jnp.int32)
    size_all = kind_count * capacity
    target = jnp.where(op_ids >= 0, op_ids * capacity + rank_ids, size_all).astype(jnp.int32)
    packed = (
        jnp.zeros((size_all,) + tile_set.shape[1:], jnp.float32)
        .at[target]
        .set(tile_set, mode="drop")
    )
    packed_rows = jnp.zeros((size_all,), jnp.int32).at[target].set(row_ids, mode="drop")
    packed_cols = jnp.zeros((size_all,), jnp.int32).at[target].set(col_ids, mode="drop")
    return (
        packed.reshape((kind_count, capacity) + tile_set.shape[1:]),
        packed_rows.reshape(kind_count, capacity),
        packed_cols.reshape(kind_count, capacity),
    )


def local(state, tile_vals, tile_row, tile_col, tile_op):
    row_total = lax.axis_size("row")
    row_place = lax.axis_index("row")
    col_place = lax.axis_index("col")
    tile_edge = tile_vals.shape[-1]
    rows_dev = state.shape[1]
    cols_dev = state.shape[2]
    row_tiles = rows_dev // tile_edge
    col_tiles = cols_dev // tile_edge
    kind_count = NOPS + 1
    block_count = NOPS // 4
    group_vals, group_rows, group_cols, group_ops = (
        lax.all_gather(tile_vals, "col", axis=0, tiled=True),
        lax.all_gather(tile_row, "col", axis=0, tiled=True),
        lax.all_gather(tile_col, "col", axis=0, tiled=True),
        lax.all_gather(tile_op, "col", axis=0, tiled=True),
    )
    slab_ids = group_rows // row_tiles
    position = jnp.arange(slab_ids.shape[0], dtype=jnp.int32)
    earlier = (slab_ids[:, None] == slab_ids[None, :]) & (position[None, :] < position[:, None])
    target = slab_ids * CAP + jnp.sum(earlier.astype(jnp.int32), axis=1, dtype=jnp.int32)
    slot_count = row_total * CAP
    bucket_vals = (
        jnp.zeros((slot_count,) + group_vals.shape[1:], jnp.float32).at[target].set(group_vals)
    )
    bucket_rows = jnp.zeros((slot_count,), jnp.int32).at[target].set(group_rows)
    bucket_cols = jnp.zeros((slot_count,), jnp.int32).at[target].set(group_cols)
    bucket_ops = jnp.full((slot_count,), -1, jnp.int32).at[target].set(group_ops)
    left_vals, left_rows, left_cols, left_ops = (
        lax.all_to_all(bucket_vals, "row", split_axis=0, concat_axis=0, tiled=True),
        lax.all_to_all(bucket_rows, "row", split_axis=0, concat_axis=0, tiled=True),
        lax.all_to_all(bucket_cols, "row", split_axis=0, concat_axis=0, tiled=True),
        lax.all_to_all(bucket_ops, "row", split_axis=0, concat_axis=0, tiled=True),
    )
    halves = []
    for offset in range(2):
        halves.append(
            (
                from_root(left_vals, "row", 2 * col_place + offset),
                from_root(left_rows, "row", 2 * col_place + offset),
                from_root(left_cols, "row", 2 * col_place + offset),
                from_root(left_ops, "row", 2 * col_place + offset),
            )
        )
    right_vals = jnp.concatenate([halves[0][0], halves[1][0]], axis=0)
    right_rows = jnp.concatenate([halves[0][1], halves[1][1]], axis=0)
    right_cols = jnp.concatenate([halves[0][2], halves[1][2]], axis=0)
    right_ops = jnp.concatenate([halves[0][3], halves[1][3]], axis=0)
    left_tiles, left_grow, left_gcol = compact(
        left_vals, left_rows, left_cols, left_ops, CAP, kind_count
    )
    right_tiles, right_grow, right_gcol = compact(
        right_vals, right_rows, right_cols, right_ops, 2 * CAP, kind_count
    )
    left_dst = jnp.clip(left_grow - row_place * row_tiles, 0, row_tiles - 1)
    left_src = jnp.clip(left_gcol - row_place * row_tiles, 0, row_tiles)
    right_dst = jnp.clip(right_grow - col_place * col_tiles, 0, col_tiles - 1)
    right_src = jnp.clip(right_gcol - col_place * col_tiles, 0, col_tiles)
    jump_inputs = (
        left_tiles[:NOPS].reshape((block_count, 4) + left_tiles.shape[1:]),
        left_src[:NOPS].reshape(block_count, 4, CAP),
        right_tiles[:NOPS].reshape((block_count, 4) + right_tiles.shape[1:]),
        right_src[:NOPS].reshape(block_count, 4, 2 * CAP),
    )
    all_to_rows = left_dst[:NOPS].reshape(block_count, 4, CAP)
    all_to_cols = right_dst[:NOPS].reshape(block_count, 4, 2 * CAP)
    ham_left_tiles = jnp.moveaxis(left_tiles[NOPS], 1, 0)
    ham_right_adj = adjoint(jnp.moveaxis(right_tiles[NOPS], 1, 0))

    def rate_of(current):
        under_rim = passed_along(current[:, :tile_edge, :], "row", -1)
        taller = jnp.concatenate([current, under_rim], axis=1)
        side_rim = passed_along(taller[:, :, :tile_edge], "col", -1)
        extended = jnp.concatenate([taller, side_rim], axis=2)
        ext_width = cols_dev + tile_edge
        row_strips = extended.reshape(2, row_tiles + 1, tile_edge, ext_width)
        rate_sum = jnp.zeros_like(current)
        ham_strips = row_strips[:, left_src[NOPS], :, :cols_dev]
        ham_left = times_minus_i(complex_product("cij,cjn->cin", ham_left_tiles, ham_strips))
        rate_sum = (
            rate_sum.reshape(2, row_tiles, tile_edge, cols_dev)
            .at[:, left_dst[NOPS]]
            .add(ham_left)
            .reshape(current.shape)
        )
        own_rows = extended[:, :rows_dev, :].reshape(2, rows_dev, col_tiles + 1, tile_edge)
        ham_cols = own_rows[:, :, right_src[NOPS], :]
        ham_right = times_i(complex_product("nbj,bjk->nbk", ham_cols, ham_right_adj))
        rate_sum = (
            rate_sum.reshape(2, rows_dev, col_tiles, tile_edge)
            .at[:, :, right_dst[NOPS]]
            .add(ham_right)
            .reshape(current.shape)
        )
        grid_ext = extended.reshape(2, row_tiles + 1, tile_edge, col_tiles + 1, tile_edge)

        def jump_block(packed):
            block_left, block_from, block_right, right_from = packed
            panels = grid_ext[:, block_from[:, :, None], :, right_from[:, None, :], :]
            panels = jnp.moveaxis(panels, 3, 0)
            comp_left = jnp.moveaxis(block_left, 2, 0)
            chosen = complex_product("ocij,ocfjw->ocfiw", comp_left, panels)
            right_adj = adjoint(jnp.moveaxis(block_right, 2, 0))
            return complex_product("ocfiw,ofwk->ocfik", chosen, right_adj)

        stacked = lax.map(jump_block, jump_inputs)
        placed = jnp.transpose(stacked, (0, 2, 3, 4, 1, 5, 6))
        grid_view = rate_sum.reshape(2, row_tiles, tile_edge, col_tiles, tile_edge)
        grid_view = grid_view.at[
            :, all_to_rows[:, :, :, None], :, all_to_cols[:, :, None, :], :
        ].add(placed)
        return grid_view.reshape(current.shape)

    first_rate = rate_of(state)
    middle = state + 0.5 * TIME_STEP * first_rate
    second_rate = rate_of(middle)
    return state + TIME_STEP * second_rate


def solution(mesh):
    placed = (
        P(None, "row", "col"),
        P(("row", "col"), None, None, None),
        P(("row", "col")),
        P(("row", "col")),
        P(("row", "col")),
    )
    return jax.shard_map(
        local, mesh=mesh, in_specs=placed, out_specs=P(None, "row", "col"), check_vma=False
    )
```

profile of v0, /device:TPU:5, one launch (start us, length us, event | category | flops | bytes accessed | tf_op | source)
XLA Modules:
  0.0 1282.0 jit_solution(6865872519024202294)
XLA Ops:
  16.7 5.8 all-to-all-start.1
  27.6 11.7 constant_dynamic-update-slice_fusion.3
  41.9 7.0 all-to-all-start.3
  50.2 25.2 %all-to-all-done.3 = s32[8,2,1]{1,2,0:T(1,128)S(1)} async-done(((s32[8,2,1]{1,2,0:T(1,128)}), s32[8,2,1]{1,2,0:T(1,128)S(1)}, u32[]{:S(2)}, u32[]{:S(2)}) %all-to-all-start.3) | async-done | bytes 96 | tf_op jit(solution)/shard_map/all_to_all | solution.py:104
  84.9 5.7 all-reduce.4
  110.4 9.6 collective-permute-start.1
  121.5 12.7 collective-permute-done.1
  134.2 11.6 fusion.74
  145.8 18.3 %copy.180 = f32[2,1024,2176]{1,2,0:T(8,128)} copy(f32[2,1024,2176]{2,1,0:T(8,128)} %fusion.74) | data formatting | bytes 35651584 | tf_op jit(solution)/shard_map/slice | solution.py:158
  164.1 18.3 %copy.181 = f32[2,1024,17,128]{3,1,2,0:T(8,128)} copy(f32[2,1024,17,128]{1,3,2,0:T(8,128)} %bitcast.636) | data formatting | bytes 35651584 | tf_op jit(solution)/shard_map/reshape | solution.py:158
  182.5 8.9 gather_fusion.2
  198.4 15.0 %pad_maximum_fusion = f32[2,1152,2176]{2,1,0:T(8,128)} fusion(f32[2,1152,128]{2,1,0:T(8,128)S(1)} %collective-permute-done.1, f32[2,1152,2048]{2,1,0:T(8,128)} %constant_dynamic-update-slice_fusion.2), kind=kLoop, calls=%fused_computation.125 | loop fusion | flops 5013504 | bytes 40108032 | tf_op jit(solution)/shard_map/concatenate | solution.py:146
  213.4 24.1 %reshape.467 = f32[2,9,128,17,128]{4,3,2,1,0:T(8,128)} reshape(f32[2,1152,2176]{2,1,0:T(8,128)} %pad_maximum_fusion) | data formatting | bytes 40108032 | tf_op jit(solution)/shard_map/reshape | solution.py:167
  237.5 19.0 %copy.187 = f32[2,9,128,17,128]{4,2,3,1,0:T(8,128)} copy(f32[2,9,128,17,128]{4,3,2,1,0:T(8,128)} %reshape.467) | data formatting | bytes 40108032 | tf_op jit(solution)/shard_map/while | solution.py:178
  258.9 10.7 while.24
  291.0 8.3 broadcast.324.clone
  299.3 8.4 scatter_fusion.2
  307.8 9.6 copy.242
  317.4 11.2 copy.183
  330.9 23.7 %all-reduce.9.cloned.1.call-done = (f32[16,2,128,128]{3,2,1,0:T(8,128)}, f32[16,2,128,128]{3,2,1,0:T(8,128)}) async-done(((f32[16,2,128,128]{3,2,1,0:T(8,128)}, f32[16,2,128,128]{3,2,1,0:T(8,128)}), (f32[16,2,128,128]{3,2,1,0:T(8,128)}, f32[16,2,128,128]{3,2,1,0:T(8,128)})) %all-reduce.9.cloned.1.call-update) | async-done | bytes 4194320 | tf_op jit(solution)/shard_map/psum | solution.py:14
  363.9 8.0 scatter_fusion.3
  393.0 8.6 scatter_fusion.4
  401.6 11.6 copy.190
  413.2 7.8 copy.185
  421.0 8.3 broadcast.345.clone2
  429.3 187.7 %while.22 = (s32[]{:T(128)}, f32[4,2,4,2,4,128,128]{6,5,1,4,3,2,0:T(8,128)}, f32[4,4,4,2,128,128]{5,4,2,1,3,0:T(8,128)}, s32[4,4,2]{1,2,0:T(2,128)}, s32[4,4,4]{...) while((s32[]{:T(128)}, ...), condition=%wide.region_24.25_spmd, body=%wide.region_23.24_spmd.sunk | while | flops 4837998592 | bytes 117442144 | solution.py:178
  431.0 9.4 gather_fusion
  440.5 5.6 copy.282
  477.8 9.4 gather_fusion
  524.6 9.4 gather_fusion
  571.4 9.4 gather_fusion
  617.0 37.3 %scatter_fusion.5 = f32[2,8,128,16,128]{4,2,3,1,0:T(8,128)} fusion(f32[2,8,128,16,128]{4,2,3,1,0:T(8,128)} %copy.190, s32[128]{0:T(128)S(1)} %copy-done.4, f32[128,2,128,128]{3,2,1,0:T(8,128)} %bitcast.639), kind=kCustom, calls=%fused_computation.16 | custom fusion | flops 4194304 | bytes 50332672 | tf_op jit(solution)/shard_map/scatter-add | solution.py:183
  654.3 6.6 broadcast_multiply_fusion.1
  660.9 11.8 copy.191
  672.8 18.0 %mul.75 = f32[2,1024,2048]{2,1,0:T(8,128)} reshape(f32[2,8,128,16,128]{4,3,2,1,0:T(8,128)} %copy.191) | data formatting | bytes 33554432 | tf_op jit(solution)/shard_map/mul | solution.py:187
  690.8 11.6 add.257
  704.8 47.2 %collective-permute-done.2 = f32[2,128,2048]{2,1,0:T(8,128)S(1)} collective-permute-done((f32[2,128,2048]{2,1,0:T(8,128)S(1)}, f32[2,128,2048]{2,1,0:T(8,128)S(1)}, u32[]{:S(2)}, u32[]{:S(2)}) %collective-permute-start.2) | collective-permute-done | bytes 2097184 | tf_op jit(solution)/shard_map/ppermute | solution.py:20
  756.6 15.1 %collective-permute-done.3 = f32[2,1152,128]{2,1,0:T(8,128)S(1)} collective-permute-done((f32[2,1152,128]{2,1,0:T(8,128)}, f32[2,1152,128]{2,1,0:T(8,128)S(1)}, u32[]{:S(2)}, u32[]{:S(2)}) %collective-permute-start.3) | collective-permute-done | bytes 1179680 | tf_op jit(solution)/shard_map/ppermute | solution.py:20
  771.7 8.5 pad_maximum_fusion.1
  780.2 6.8 copy-done.2
  787.0 6.4 slice.264
  793.4 18.3 %copy.195 = f32[2,1024,2176]{1,2,0:T(8,128)} copy(f32[2,1024,2176]{2,1,0:T(8,128)} %slice.264) | data formatting | bytes 35651584 | tf_op jit(solution)/shard_map/slice | solution.py:158
  811.7 18.3 %copy.196 = f32[2,1024,17,128]{3,1,2,0:T(8,128)} copy(f32[2,1024,17,128]{1,3,2,0:T(8,128)} %bitcast.637) | data formatting | bytes 35651584 | tf_op jit(solution)/shard_map/reshape | solution.py:158
  830.0 9.0 gather_fusion.3
  851.8 11.1 while.25
  873.6 24.0 %reshape.471 = f32[2,9,128,17,128]{4,3,2,1,0:T(8,128)} reshape(f32[2,1152,2176]{2,1,0:T(8,128)} %bitcast.630) | data formatting | bytes 40108032 | tf_op jit(solution)/shard_map/reshape | solution.py:167
  911.3 8.3 broadcast.324
  919.6 8.0 scatter_fusion.6
  927.7 9.4 copy.243
  937.1 10.8 copy.198
  947.8 8.6 scatter_fusion.7
  956.5 11.8 copy.205
  968.2 18.9 %copy.202 = f32[2,9,128,17,128]{4,2,3,1,0:T(8,128)} copy(f32[2,9,128,17,128]{4,3,2,1,0:T(8,128)} %reshape.471) | data formatting | bytes 40108032 | tf_op jit(solution)/shard_map/while | solution.py:178
  987.1 8.3 broadcast.345.clone
  995.4 187.6 %while.23 = (s32[]{:T(128)}, f32[4,2,4,2,4,128,128]{6,5,1,4,3,2,0:T(8,128)}, f32[4,4,4,2,128,128]{5,4,2,1,3,0:T(8,128)}, s32[4,4,2]{1,2,0:T(2,128)}, s32[4,4,4]{...) while((s32[]{:T(128)}, ...), condition=%wide.region_29.30_spmd, body=%wide.region_28.29_spmd.sunk | while | flops 4837998592 | bytes 117442144 | solution.py:178
  997.2 9.4 gather_fusion.1
  1044.0 9.4 gather_fusion.1
  1090.8 9.4 gather_fusion.1
  1137.6 9.4 gather_fusion.1
  1183.0 37.7 %scatter_fusion.8 = f32[2,8,128,16,128]{4,2,3,1,0:T(8,128)} fusion(f32[2,8,128,16,128]{4,2,3,1,0:T(8,128)} %copy.205, s32[128]{0:T(128)S(1)} %copy-done.5, f32[128,2,128,128]{3,2,1,0:T(8,128)} %bitcast.638), kind=kCustom, calls=%fused_computation.19 | custom fusion | flops 4194304 | bytes 50332672 | tf_op jit(solution)/shard_map/scatter-add | solution.py:183
  1220.8 6.6 broadcast_multiply_fusion
  1227.4 11.8 copy.206
  1239.2 18.0 %mul.78 = f32[2,1024,2048]{2,1,0:T(8,128)} reshape(f32[2,8,128,16,128]{4,3,2,1,0:T(8,128)} %copy.206) | data formatting | bytes 33554432 | tf_op jit(solution)/shard_map/mul | solution.py:189
  1257.2 17.5 %add.260 = f32[2,1024,2048]{2,1,0:T(8,128)} add(f32[2,1024,2048]{2,1,0:T(8,128)} %param.9, f32[2,1024,2048]{2,1,0:T(8,128)} %mul.78) | non-fusion elementwise | flops 4194304 | bytes 50331648 | tf_op jit(solution)/shard_map/add | solution.py:189
  (340 shorter events, 470.6 us)
Async XLA Ops:
  16.7 25.2 %all-to-all-start.1 = ((s32[8,2,1]{1,2,0:T(1,128)}), s32[8,2,1]{1,2,0:T(1,128)S(1)}, u32[]{:S(2)}, u32[]{:S(2)}) async-start(s32[8,2,1]{1,2,0:T(1,128)} %bitcast.80), calls=%async_computation.1 | async-start | bytes 8192 | tf_op jit(solution)/shard_map/all_to_all | solution.py:103
  22.5 71.4 %all-gather.2.cloned.1.call-start = ((), (), s32[]{:S(2)}) async-start(), calls=%async_computation.4 | async-start | bytes 1310720 | tf_op jit(solution)/shard_map/all_gather | solution.py:85
  25.6 79.2 %collective-permute-start = (f32[2,128,2048]{2,1,0:T(8,128)}, f32[2,128,2048]{2,1,0:T(8,128)}, u32[]{:S(2)}, u32[]{:S(2)}) collective-permute-start(f32[2,128,2048]{2,1,0:T(8,128)} %slice.168), channel_id=1, source_target_pairs={{4,0},{8,4},{12,8},{16,12},{20,16},{24,20},{28,24},{5,1},{9,5},{13... | collective-permute-start | bytes 6291464 | tf_op jit(solution)/shard_map/ppermute | solution.py:20
  41.9 33.4 %all-to-all-start.3 = ((s32[8,2,1]{1,2,0:T(1,128)}), s32[8,2,1]{1,2,0:T(1,128)S(1)}, u32[]{:S(2)}, u32[]{:S(2)}) async-start(s32[8,2,1]{1,2,0:T(1,128)} %bitcast.87), calls=%async_computation.3 | async-start | bytes 8192 | tf_op jit(solution)/shard_map/all_to_all | solution.py:104
  75.3 7.6 all-to-all-start
  93.9 1.5 copy-start.15
  98.3 97.6 %all-to-all-start.2 = ((f32[16,2,128,128]{3,2,1,0:T(8,128)}), f32[16,2,128,128]{3,2,1,0:T(8,128)S(1)}, u32[]{:S(2)}, u32[]{:S(2)}) async-start(f32[16,2,128,128]{3,2,1,0:T(8,128)} %scatter_fusion), calls=%async_computation.2 | async-start | bytes 4194304 | tf_op jit(solution)/shard_map/all_to_all | solution.py:102
  103.8 250.8 %all-reduce.9.cloned.1.call-start = ((), (), s32[]{:S(2)}) async-start(), calls=%async_computation.5 | async-start | bytes 8388608 | tf_op jit(solution)/shard_map/psum | solution.py:14
  110.4 23.8 %collective-permute-start.1 = (f32[2,1152,128]{2,1,0:T(8,128)}, f32[2,1152,128]{2,1,0:T(8,128)S(1)}, u32[]{:S(2)}, u32[]{:S(2)}) collective-permute-start(f32[2,1152,128]{2,1,0:T(8,128)} %slice.249), channel_id=1, source_target_pairs={{1,0},{2,1},{3,2},{5,4},{6,5},{7,6},{9,8},{10,9},{11,10},{13,12},{... | collective-permute-start | bytes 3538952 | tf_op jit(solution)/shard_map/ppermute | solution.py:20
  120.8 61.6 %copy-start.16 = (s32[1024]{0:T(1024)}, s32[1024]{0:T(1024)S(1)}, u32[]{:S(2)}) copy-start(s32[1024]{0:T(1024)S(1)} %pad_clamp_fusion) | copy-start | bytes 12292
  120.9 178.4 %copy-start.19 = (s32[2]{0:T(128)}, s32[2]{0:T(128)S(1)}, u32[]{:S(2)}) copy-start(s32[2]{0:T(128)S(1)} %fusion.116) | copy-start | bytes 28
  269.7 2.7 copy-start.21
  276.2 5.8 copy-start.7
  282.0 3.9 copy-start.13
  317.4 11.2 copy-start.9
  371.9 5.1 copy-start.6
  373.1 5.9 copy-start.10
  373.1 8.4 slice-start
  377.0 4.5 slice-start.1
  379.0 2.6 slice-start.2
  387.6 5.4 copy-start.17
  429.3 187.7 %copy-start.4 = (s32[128]{0:T(128)S(1)}, s32[128]{0:T(128)}, u32[]{:S(2)}) copy-start(s32[128]{0:T(128)} %reshape.642) | copy-start | bytes 1540
  447.4 3.7 copy-start
  494.2 3.7 copy-start
  541.0 3.7 copy-start
  587.8 3.7 copy-start
  702.4 50.7 %copy-start.3 = (f32[2,1024,2048]{2,1,0:T(8,128)}, f32[2,1024,2048]{2,1,0:T(8,128)S(1)}, u32[]{:S(2)}) copy-start(f32[2,1024,2048]{2,1,0:T(8,128)S(1)} %add.257) | copy-start | bytes 50331652
  702.7 49.3 %collective-permute-start.2 = (f32[2,128,2048]{2,1,0:T(8,128)S(1)}, f32[2,128,2048]{2,1,0:T(8,128)S(1)}, u32[]{:S(2)}, u32[]{:S(2)}) collective-permute-start(f32[2,128,2048]{2,1,0:T(8,128)S(1)} %slice.261), channel_id=1, source_target_pairs={{4,0},{8,4},{12,8},{16,12},{20,16},{24,20},{28,24},{5,1},{9,5},{13... | collective-permute-start | bytes 6291464 | tf_op jit(solution)/shard_map/ppermute | solution.py:20
  753.1 18.6 %collective-permute-start.3 = (f32[2,1152,128]{2,1,0:T(8,128)}, f32[2,1152,128]{2,1,0:T(8,128)S(1)}, u32[]{:S(2)}, u32[]{:S(2)}) collective-permute-start(f32[2,1152,128]{2,1,0:T(8,128)} %pad_maximum_fusion.3), channel_id=1, source_target_pairs={{1,0},{2,1},{3,2},{5,4},{6,5},{7,6},{9,8},{10,9},{11,10},{13,12},{... | collective-permute-start | bytes 3538952 | tf_op jit(solution)/shard_map/ppermute | solution.py:20
  780.2 6.8 copy-start.2
  839.0 2.6 copy-start.11
  849.3 2.5 copy-start.22
  851.8 11.1 copy-start.14
  862.9 3.6 copy-start.8
  901.6 5.5 copy-start.12
  911.3 8.3 copy-start.20
  937.1 10.8 copy-start.18
  995.4 187.6 %copy-start.5 = (s32[128]{0:T(128)S(1)}, s32[128]{0:T(128)}, u32[]{:S(2)}) copy-start(s32[128]{0:T(128)} %reshape.642) | copy-start | bytes 1540
  1013.6 3.7 copy-start.1
  1060.4 3.7 copy-start.1
  1107.2 3.7 copy-start.1
  1154.0 3.7 copy-start.1
Sparse Core Ops, SparseCore 0:
  27.7 20.3 all-gather.1
  198.5 156.0 all-reduce.8
where the time goes:
time: 1300 us; the launch traced here: 1280 us
  local copies, waits for them, and re-layouts  702 us (54%)
  other arithmetic  243 us (19%)
  matrix products  144 us (11%)
  waiting for transfers between devices  127 us (10%)
  starting transfers between devices  38.8 us (3%)
  between operations  15.2 us (1%)
    gather x16, local copies, waits for them, and re-layouts, jump_block(): panels = grid_ext[:, block_from[:, :, None], :, right_from[:, None, :], :]  121 us
    dynamic_update_slice x16, local copies, waits for them, and re-layouts, rate_of(): stacked = lax.map(jump_block, jump_inputs)  79.4 us
    scatter-add x2, other arithmetic, rate_of(): grid_view = grid_view.at[:, all_to_rows[:, :, :, None], :, all_to_cols[:,...  75 us
    ppermute x4, waiting for transfers between devices, passed_along(): return lax.ppermute(block, axis, route)  74.9 us
    dot_general x20, matrix products, complex_product(): jnp.einsum(formula, left_part[1], right_part[1], precision=PRECISE, prefe...  54.6 us
    while x5, local copies, waits for them, and re-layouts, rate_of(): stacked = lax.map(jump_block, jump_inputs)  48.6 us
    dot_general x20, matrix products, complex_product(): jnp.einsum(formula, left_part[0] + left_part[1], right_part[0] + right_pa...  48.5 us
    reshape x2, local copies, waits for them, and re-layouts, rate_of(): extended.reshape(2, row_tiles + 1, tile_edge, col_tiles + 1, tile_edge)  48.1 us
  transfers between devices with their start and end apart: 10, of which 6 were waited for; matrix products, arithmetic and copies ran while one was open for 18% of the time, Pallas kernels for 0%

commit v1 on v0

--- a/solution.py
+++ b/solution.py
@@ -11,7 +11,7 @@
 
 def from_root(value, axis, source):
     kept = jnp.where(lax.axis_index(axis) == source, value, 0).astype(value.dtype)
-    return lax.psum(kept, axis)
+    return jnp.sum(lax.all_gather(kept, axis), axis=0)
 
 
 def passed_along(block, axis, distance):

time: 1300 us -> 1540 us (1.18)
  waiting for transfers between devices: 127 us -> 245 us
  blocking collectives: 9.9 us -> 95.2 us
  other arithmetic: 243 us -> 261 us
  starting transfers between devices: 38.8 us -> 56.5 us
    all_gather x0 -> x6, blocking collectives: none -> 91 us  [from_root(): return jnp.sum(lax.all_gather(kept, axis), axis=0)]
    all_to_all x1, waiting for transfers between devices: 25.2 us -> 90.6 us  [local(): lax.all_to_all(bucket_cols, 'row', split_axis=0, concat_axis=0, tiled=True)]
    all_to_all x1, waiting for transfers between devices: 0.01 us -> 47.5 us  [local(): lax.all_to_all(bucket_vals, 'row', split_axis=0, concat_axis=0, tiled=True)]
    psum x1 -> x0, waiting for transfers between devices: 23.7 us -> none  [from_root(): return lax.psum(kept, axis)]
    ppermute x4, starting transfers between devices: 17.1 us -> 35.9 us  [passed_along(): return lax.ppermute(block, axis, route)]
    all_gather x0 -> x2, waiting for transfers between devices: none -> 17.4 us  [from_root(): return jnp.sum(lax.all_gather(kept, axis), axis=0)]
    reduce_sum x0 -> x8, other arithmetic: none -> 17.1 us  [from_root(): return jnp.sum(lax.all_gather(kept, axis), axis=0)]
    unnamed x61 -> x67, local copies, waits for them, and re-layouts: 46.5 us -> 47.1 us
  transfers between devices with their start and end apart: 10 -> 11, of which waited for: 6 -> 8; matrix products, arithmetic and copies ran while one was open for 18% -> 16% of each run, Pallas kernels for 0% -> 0%
where the time goes in v1:
time: 1540 us; the launch traced here: 1520 us
  local copies, waits for them, and re-layouts  703 us (46%)
  other arithmetic  261 us (17%)
  waiting for transfers between devices  245 us (16%)
  matrix products  144 us (9%)
  blocking collectives  95.2 us (6%)
  starting transfers between devices  56.5 us (4%)
    gather x16, local copies, waits for them, and re-layouts, jump_block(): panels = grid_ext[:, block_from[:, :, None], :, right_from[:, None, :], :]  121 us
    all_gather x6, blocking collectives, from_root(): return jnp.sum(lax.all_gather(kept, axis), axis=0)  91 us
    all_to_all x1, waiting for transfers between devices, local(): lax.all_to_all(bucket_cols, 'row', split_axis=0, concat_axis=0, tiled=True)  90.6 us
    dynamic_update_slice x16, local copies, waits for them, and re-layouts, rate_of(): stacked = lax.map(jump_block, jump_inputs)  79.5 us
    scatter-add x2, other arithmetic, rate_of(): grid_view = grid_view.at[:, all_to_rows[:, :, :, None], :, all_to_cols[:,...  75.2 us
    ppermute x4, waiting for transfers between devices, passed_along(): return lax.ppermute(block, axis, route)  74.6 us
    dot_general x20, matrix products, complex_product(): jnp.einsum(formula, left_part[1], right_part[1], precision=PRECISE, prefe...  54.6 us
    while x5, local copies, waits for them, and re-layouts, rate_of(): stacked = lax.map(jump_block, jump_inputs)  48.6 us
  transfers between devices with their start and end apart: 11, of which 8 were waited for; matrix products, arithmetic and copies ran while one was open for 16% of the time, Pallas kernels for 0%

profile of v1, /device:TPU:5, one launch (start us, length us, event | category | flops | bytes accessed | tf_op | source)
XLA Modules:
  0.0 1522.0 jit_solution(12149177927398328174)
XLA Ops:
  16.2 11.1 all-gather.12.cloned.1.call-done
  37.2 47.5 %all-to-all-done.2 = f32[16,2,128,128]{3,2,1,0:T(8,128)S(1)} async-done(((f32[16,2,128,128]{3,2,1,0:T(8,128)}), f32[16,2,128,128]{3,2,1,0:T(8,128)S(1)}, u32[]{:S(2)}, u32[]{:S(2)}) %all-to-all-start.2) | async-done | bytes 2097184 | tf_op jit(solution)/shard_map/all_to_all | solution.py:102
  100.5 11.8 constant_dynamic-update-slice_fusion.3
  121.9 90.6 %all-to-all-done.3 = s32[8,2,1]{1,2,0:T(1,128)S(1)} async-done(((s32[8,2,1]{1,2,0:T(1,128)}), s32[8,2,1]{1,2,0:T(1,128)S(1)}, u32[]{:S(2)}, u32[]{:S(2)}) %all-to-all-start.3) | async-done | bytes 96 | tf_op jit(solution)/shard_map/all_to_all | solution.py:104
  221.2 14.9 all-gather.2
  236.1 14.1 all-gather.3
  250.2 16.4 %all-gather.6 = s32[8,1,16]{2,1,0:T(1,128)S(1)} all-gather(s32[1,1,16]{2,1,0:T(1,128)S(1)} %reshape.771), channel_id=1, replica_groups=mesh['row'=8,'col'=4] {'row'}, dimensions={0}, use_global_device_ids=true | all-gather | bytes 576 | tf_op jit(solution)/shard_map/all_gather | solution.py:14
  266.6 16.8 %all-gather.7 = s32[8,1,16]{2,1,0:T(1,128)S(1)} all-gather(s32[1,1,16]{2,1,0:T(1,128)S(1)} %reshape.773), channel_id=1, replica_groups=mesh['row'=8,'col'=4] {'row'}, dimensions={0}, use_global_device_ids=true | all-gather | bytes 576 | tf_op jit(solution)/shard_map/all_gather | solution.py:14
  286.1 14.4 all-gather.4
  300.5 14.4 all-gather.5
  322.2 27.3 %collective-permute-start.1 = (f32[2,1152,128]{2,1,0:T(8,128)}, f32[2,1152,128]{2,1,0:T(8,128)S(1)}, u32[]{:S(2)}, u32[]{:S(2)}) collective-permute-start(f32[2,1152,128]{2,1,0:T(8,128)} %slice.249), channel_id=1, source_target_pairs={{1,0},{2,1},{3,2},{5,4},{6,5},{7,6},{9,8},{10,9},{11,10},{13,12},{... | collective-permute-start | bytes 3538952 | tf_op jit(solution)/shard_map/ppermute | solution.py:20
  351.1 13.6 collective-permute-done.1
  364.7 13.1 fusion.74
  377.8 18.3 %copy.180 = f32[2,1024,2176]{1,2,0:T(8,128)} copy(f32[2,1024,2176]{2,1,0:T(8,128)} %fusion.74) | data formatting | bytes 35651584 | tf_op jit(solution)/shard_map/slice | solution.py:158
  396.1 18.4 %copy.181 = f32[2,1024,17,128]{3,1,2,0:T(8,128)} copy(f32[2,1024,17,128]{1,3,2,0:T(8,128)} %bitcast.638) | data formatting | bytes 35651584 | tf_op jit(solution)/shard_map/reshape | solution.py:158
  414.5 9.0 gather_fusion.2
  428.0 14.8 pad_maximum_fusion
  442.8 23.6 %reshape.545 = f32[2,9,128,17,128]{4,3,2,1,0:T(8,128)} reshape(f32[2,1152,2176]{2,1,0:T(8,128)} %pad_maximum_fusion) | data formatting | bytes 40108032 | tf_op jit(solution)/shard_map/reshape | solution.py:167
  466.4 18.9 %copy.187 = f32[2,9,128,17,128]{4,2,3,1,0:T(8,128)} copy(f32[2,9,128,17,128]{4,3,2,1,0:T(8,128)} %reshape.545) | data formatting | bytes 40108032 | tf_op jit(solution)/shard_map/while | solution.py:178
  487.8 10.9 while.24
  520.2 8.3 broadcast.423.clone
  528.5 8.0 scatter_fusion.2
  536.5 9.8 copy.244
  546.3 11.0 copy.183
  567.3 17.4 %all-gather.16.cloned.1.call-done = f32[128,2,128,128]{3,2,1,0:T(8,128)} async-done(((f32[16,2,128,128]{3,2,1,0:T(8,128)}), f32[128,2,128,128]{3,2,1,0:T(8,128)}) %all-gather.16.cloned.1.call-update) | async-done | bytes 16777232 | tf_op jit(solution)/shard_map/all_gather | solution.py:14
  584.7 9.1 reduce_sum.113
  602.4 8.4 scatter_fusion.3
  631.9 8.6 scatter_fusion.4
  640.5 11.6 copy.190
  659.9 8.3 broadcast.444.clone2
  668.2 187.8 %while.22 = (s32[]{:T(128)}, f32[4,2,4,2,4,128,128]{6,5,1,4,3,2,0:T(8,128)}, f32[4,4,4,2,128,128]{5,4,2,1,3,0:T(8,128)}, s32[4,4,2]{1,2,0:T(2,128)}, s32[4,4,4]{...) while((s32[]{:T(128)}, ...), condition=%wide.region_24.25_spmd, body=%wide.region_23.24_spmd.sunk | while | flops 4837998592 | bytes 117442144 | solution.py:178
  670.0 9.4 gather_fusion
  716.8 9.4 gather_fusion
  763.5 9.4 gather_fusion
  810.4 9.4 gather_fusion
  856.0 37.3 %scatter_fusion.5 = f32[2,8,128,16,128]{4,2,3,1,0:T(8,128)} fusion(f32[2,8,128,16,128]{4,2,3,1,0:T(8,128)} %copy.190, s32[128]{0:T(128)S(1)} %copy-done.4, f32[128,2,128,128]{3,2,1,0:T(8,128)} %bitcast.641), kind=kCustom, calls=%fused_computation.16 | custom fusion | flops 4194304 | bytes 50332672 | tf_op jit(solution)/shard_map/scatter-add | solution.py:183
  899.9 11.8 copy.191
  911.8 18.0 %mul.75 = f32[2,1024,2048]{2,1,0:T(8,128)} reshape(f32[2,8,128,16,128]{4,3,2,1,0:T(8,128)} %copy.191) | data formatting | bytes 33554432 | tf_op jit(solution)/shard_map/mul | solution.py:187
  929.8 11.6 add.241
  944.7 46.0 %collective-permute-done.2 = f32[2,128,2048]{2,1,0:T(8,128)S(1)} collective-permute-done((f32[2,128,2048]{2,1,0:T(8,128)S(1)}, f32[2,128,2048]{2,1,0:T(8,128)S(1)}, u32[]{:S(2)}, u32[]{:S(2)}) %collective-permute-start.2) | collective-permute-done | bytes 2097184 | tf_op jit(solution)/shard_map/ppermute | solution.py:20
  995.6 15.0 collective-permute-done.3
  1010.6 8.5 pad_maximum_fusion.1
  1032.3 18.3 %copy.195 = f32[2,1024,2176]{1,2,0:T(8,128)} copy(f32[2,1024,2176]{2,1,0:T(8,128)} %slice.264) | data formatting | bytes 35651584 | tf_op jit(solution)/shard_map/slice | solution.py:158
  1050.6 18.3 %copy.196 = f32[2,1024,17,128]{3,1,2,0:T(8,128)} copy(f32[2,1024,17,128]{1,3,2,0:T(8,128)} %bitcast.639) | data formatting | bytes 35651584 | tf_op jit(solution)/shard_map/reshape | solution.py:158
  1068.9 9.0 gather_fusion.3
  1090.8 11.1 while.25
  1112.5 24.0 %reshape.549 = f32[2,9,128,17,128]{4,3,2,1,0:T(8,128)} reshape(f32[2,1152,2176]{2,1,0:T(8,128)} %bitcast.632) | data formatting | bytes 40108032 | tf_op jit(solution)/shard_map/reshape | solution.py:167
  1150.4 8.3 broadcast.423
  1158.7 8.0 scatter_fusion.6
  1166.7 9.4 copy.245
  1176.2 10.8 copy.198
  1186.9 8.6 scatter_fusion.7
  1195.5 11.8 copy.205
  1207.3 18.9 %copy.202 = f32[2,9,128,17,128]{4,2,3,1,0:T(8,128)} copy(f32[2,9,128,17,128]{4,3,2,1,0:T(8,128)} %reshape.549) | data formatting | bytes 40108032 | tf_op jit(solution)/shard_map/while | solution.py:178
  1226.2 8.3 broadcast.444.clone
  1234.5 188.5 %while.23 = (s32[]{:T(128)}, f32[4,2,4,2,4,128,128]{6,5,1,4,3,2,0:T(8,128)}, f32[4,4,4,2,128,128]{5,4,2,1,3,0:T(8,128)}, s32[4,4,2]{1,2,0:T(2,128)}, s32[4,4,4]{...) while((s32[]{:T(128)}, ...), condition=%wide.region_29.30_spmd, body=%wide.region_28.29_spmd.sunk | while | flops 4837998592 | bytes 117442144 | solution.py:178
  1236.3 9.5 gather_fusion.1
  1283.4 9.5 gather_fusion.1
  1330.3 9.5 gather_fusion.1
  1377.4 9.5 gather_fusion.1
  1423.1 37.9 %scatter_fusion.8 = f32[2,8,128,16,128]{4,2,3,1,0:T(8,128)} fusion(f32[2,8,128,16,128]{4,2,3,1,0:T(8,128)} %copy.205, s32[128]{0:T(128)S(1)} %copy-done.5, f32[128,2,128,128]{3,2,1,0:T(8,128)} %bitcast.640), kind=kCustom, calls=%fused_computation.19 | custom fusion | flops 4194304 | bytes 50332672 | tf_op jit(solution)/shard_map/scatter-add | solution.py:183
  1467.6 11.8 copy.206
  1479.4 18.0 %mul.78 = f32[2,1024,2048]{2,1,0:T(8,128)} reshape(f32[2,8,128,16,128]{4,3,2,1,0:T(8,128)} %copy.206) | data formatting | bytes 33554432 | tf_op jit(solution)/shard_map/mul | solution.py:189
  1497.5 17.5 %add.244 = f32[2,1024,2048]{2,1,0:T(8,128)} add(f32[2,1024,2048]{2,1,0:T(8,128)} %param.9, f32[2,1024,2048]{2,1,0:T(8,128)} %mul.78) | non-fusion elementwise | flops 4194304 | bytes 50331648 | tf_op jit(solution)/shard_map/add | solution.py:189
  (360 shorter events, 532.4 us)
Async XLA Ops:
  6.5 20.7 %all-gather.12.cloned.1.call-start = ((), (), s32[]{:S(2)}) async-start(), calls=%async_computation.4 | async-start | bytes 1310720 | tf_op jit(solution)/shard_map/all_gather | solution.py:85
  27.3 1.6 copy-start.15
  31.7 53.0 %all-to-all-start.2 = ((f32[16,2,128,128]{3,2,1,0:T(8,128)}), f32[16,2,128,128]{3,2,1,0:T(8,128)S(1)}, u32[]{:S(2)}, u32[]{:S(2)}) async-start(f32[16,2,128,128]{3,2,1,0:T(8,128)} %scatter_fusion), calls=%async_computation.2 | async-start | bytes 4194304 | tf_op jit(solution)/shard_map/all_to_all | solution.py:102
  37.2 522.3 %all-gather.14.cloned.1.call-start = ((), (), s32[]{:S(2)}) async-start(), calls=%async_computation.5 | async-start | bytes 18874368 | tf_op jit(solution)/shard_map/all_gather | solution.py:14
  87.3 497.4 %all-gather.16.cloned.1.call-start = ((), (), s32[]{:S(2)}) async-start(), calls=%async_computation.6 | async-start | bytes 18874368 | tf_op jit(solution)/shard_map/all_gather | solution.py:14
  89.3 24.3 %all-to-all-start = ((s32[8,2,1]{1,2,0:T(1,128)}), s32[8,2,1]{1,2,0:T(1,128)S(1)}, u32[]{:S(2)}, u32[]{:S(2)}) async-start(s32[8,2,1]{1,2,0:T(1,128)} %bitcast.77), calls=%async_computation | async-start | bytes 8192 | tf_op jit(solution)/shard_map/all_to_all | solution.py:105
  97.3 219.3 %collective-permute-start = (f32[2,128,2048]{2,1,0:T(8,128)}, f32[2,128,2048]{2,1,0:T(8,128)}, u32[]{:S(2)}, u32[]{:S(2)}) collective-permute-start(f32[2,128,2048]{2,1,0:T(8,128)} %slice.168), channel_id=1, source_target_pairs={{4,0},{8,4},{12,8},{16,12},{20,16},{24,20},{28,24},{5,1},{9,5},{13... | collective-permute-start | bytes 6291464 | tf_op jit(solution)/shard_map/ppermute | solution.py:20
  113.6 98.9 %all-to-all-start.3 = ((s32[8,2,1]{1,2,0:T(1,128)}), s32[8,2,1]{1,2,0:T(1,128)S(1)}, u32[]{:S(2)}, u32[]{:S(2)}) async-start(s32[8,2,1]{1,2,0:T(1,128)} %bitcast.87), calls=%async_computation.3 | async-start | bytes 8192 | tf_op jit(solution)/shard_map/all_to_all | solution.py:104
  212.5 7.8 all-to-all-start.1
  322.2 42.5 %collective-permute-start.1 = (f32[2,1152,128]{2,1,0:T(8,128)}, f32[2,1152,128]{2,1,0:T(8,128)S(1)}, u32[]{:S(2)}, u32[]{:S(2)}) collective-permute-start(f32[2,1152,128]{2,1,0:T(8,128)} %slice.249), channel_id=1, source_target_pairs={{1,0},{2,1},{3,2},{5,4},{6,5},{7,6},{9,8},{10,9},{11,10},{13,12},{... | collective-permute-start | bytes 3538952 | tf_op jit(solution)/shard_map/ppermute | solution.py:20
  350.4 64.1 %copy-start.16 = (s32[1024]{0:T(1024)}, s32[1024]{0:T(1024)S(1)}, u32[]{:S(2)}) copy-start(s32[1024]{0:T(1024)S(1)} %pad_clamp_fusion) | copy-start | bytes 12292
  350.5 178.0 %copy-start.19 = (s32[2]{0:T(128)}, s32[2]{0:T(128)S(1)}, u32[]{:S(2)}) copy-start(s32[2]{0:T(128)S(1)} %fusion.122) | copy-start | bytes 28
  498.7 2.7 copy-start.21
  505.3 5.8 copy-start.7
  511.1 3.9 copy-start.13
  546.3 11.0 copy-start.9
  610.8 5.1 copy-start.6
  612.0 5.9 copy-start.10
  612.0 8.4 slice-start
  615.9 4.5 slice-start.1
  617.9 2.6 slice-start.2
  626.5 5.4 copy-start.17
  668.2 187.8 %copy-start.4 = (s32[128]{0:T(128)S(1)}, s32[128]{0:T(128)}, u32[]{:S(2)}) copy-start(s32[128]{0:T(128)} %reshape.720) | copy-start | bytes 1540
  686.3 3.7 copy-start
  733.2 3.7 copy-start
  779.9 3.7 copy-start
  826.8 3.7 copy-start
  941.4 50.5 %copy-start.3 = (f32[2,1024,2048]{2,1,0:T(8,128)}, f32[2,1024,2048]{2,1,0:T(8,128)S(1)}, u32[]{:S(2)}) copy-start(f32[2,1024,2048]{2,1,0:T(8,128)S(1)} %add.241) | copy-start | bytes 50331652
  941.7 49.0 %collective-permute-start.2 = (f32[2,128,2048]{2,1,0:T(8,128)S(1)}, f32[2,128,2048]{2,1,0:T(8,128)S(1)}, u32[]{:S(2)}, u32[]{:S(2)}) collective-permute-start(f32[2,128,2048]{2,1,0:T(8,128)S(1)} %slice.261), channel_id=1, source_target_pairs={{4,0},{8,4},{12,8},{16,12},{20,16},{24,20},{28,24},{5,1},{9,5},{13... | collective-permute-start | bytes 6291464 | tf_op jit(solution)/shard_map/ppermute | solution.py:20
  991.9 18.7 %collective-permute-start.3 = (f32[2,1152,128]{2,1,0:T(8,128)}, f32[2,1152,128]{2,1,0:T(8,128)S(1)}, u32[]{:S(2)}, u32[]{:S(2)}) collective-permute-start(f32[2,1152,128]{2,1,0:T(8,128)} %pad_maximum_fusion.3), channel_id=1, source_target_pairs={{1,0},{2,1},{3,2},{5,4},{6,5},{7,6},{9,8},{10,9},{11,10},{13,12},{... | collective-permute-start | bytes 3538952 | tf_op jit(solution)/shard_map/ppermute | solution.py:20
  1019.1 6.8 copy-start.2
  1078.0 2.6 copy-start.11
  1088.2 2.5 copy-start.22
  1090.7 11.1 copy-start.14
  1101.8 3.6 copy-start.8
  1140.6 5.5 copy-start.12
  1150.4 8.3 copy-start.20
  1176.2 10.8 copy-start.18
  1234.5 188.5 %copy-start.5 = (s32[128]{0:T(128)S(1)}, s32[128]{0:T(128)}, u32[]{:S(2)}) copy-start(s32[128]{0:T(128)} %reshape.720) | copy-start | bytes 1540
  1252.8 3.7 copy-start.1
  1299.9 3.7 copy-start.1
  1346.9 3.7 copy-start.1
  1393.9 3.7 copy-start.1
Sparse Core Ops, SparseCore 0:
  8.9 18.3 all-gather.11
  87.4 269.2 all-gather.13
  358.9 225.7 all-gather.15
